TPU v7x, 32 devices: a whole 2x2x4 slice. The times are simulated.
32 devices in a mesh: grp: 2 (over y), evt: 4 (over z), var: 2 (over x), chan: 2 (over core).
Axes of the slice: x: 2, y: 2, z: 4, core: 2. Of those that a mesh axis runs over, the one named last changes fastest.
Arguments:
- variation_weights: bfloat16 [2, 32768, 1024], P('chan', ('grp', 'evt'), 'var'), parts along dimension 1, may hold values from -6 to 6
- bin_response: bfloat16 [2, 32768, 128], P('chan', ('grp', 'evt')), parts along dimension 1, may hold values from 0 to 0.25
- bin_block: int32 [2, 256], P('chan', ('grp', 'evt')), parts along dimension 1, may hold values from 0 to 127
- variation_coefficient: float32 [1024], replicated, may hold values from -4 to 4
- nuisance_index: int32 [1024], replicated, may hold values from 0 to 511, as said below
- expected: float32 [2, 32768], P('chan', ('grp', 'evt', 'var')), parts along dimension 1, may hold values from 1 to 16
- excess_counts: float32 [2, 32768], P('chan', ('grp', 'evt', 'var')), parts along dimension 1, may hold values from -10 to 10
Outputs:
- templates: float32 [2, 32768, 1024], P('chan', ('grp', 'evt', 'var')), parts along dimension 1
- nuisance_pulls: float32 [1024], P('grp'), parts along dimension 0
There are 2 independent parts, one for each index of `grp`. A program takes and returns all parts, laid end to end along the dimension named above; an argument that names none is the same for every part. Nothing has to cross between parts.
Inputs may be any that keep to these rules, and one draw needn't show every extreme that they name: `nuisance_index`: each of the 512 nuisances is named by exactly 2 variations.
All inputs are finite; a program needn't handle non-finite values.
Results may differ from a plain program's by a relative error of at most 0.0085.
Values may be sent and summed in bfloat16 or wider, within the bound.
A program may use at most 128 MiB of HBM per device.

v0:
```python
import jax
import jax.numpy as jnp
from jax import lax
from jax.sharding import PartitionSpec as P

BLK = 128
CH_BINS = 16384
NUIS = 512


def shards(
    variation_weights,
    bin_response,
    bin_block,
    variation_coefficient,
    nuisance_index,
    expected,
    excess_counts,
):
    weights = variation_weights[0]
    response = bin_response[0]
    blocks = bin_block[0]
    evt_count = lax.axis_size("evt")
    nblocks = blocks.shape[0]
    var_local = weights.shape[1]
    products = jnp.einsum(
        "ket,kev->ktv",
        response.reshape(nblocks, BLK, BLK),
        weights.reshape(nblocks, BLK, var_local),
        preferred_element_type=jnp.float32,
    )
    targets = lax.iota(jnp.int32, CH_BINS // evt_count * lax.axis_size("evt") // BLK)
    select = (blocks[None, :] == targets[:, None]).astype(jnp.float32)
    block_term = jnp.einsum("qk,ktv->qtv", select, products, precision=lax.Precision.HIGHEST)
    summed = lax.psum_scatter(
        block_term.reshape(CH_BINS // evt_count * lax.axis_size("evt"), var_local).astype(
            jnp.bfloat16
        ),
        "evt",
        scatter_dimension=0,
        tiled=True,
    ).astype(jnp.float32)
    local_templates = lax.all_to_all(
        summed.astype(jnp.bfloat16), "var", split_axis=0, concat_axis=1, tiled=True
    ).astype(summed.dtype)
    mixing = (nuisance_index[:, None] == lax.iota(jnp.int32, NUIS)[None, :]).astype(
        jnp.float32
    ) * variation_coefficient[:, None]
    jacobian = jnp.dot(local_templates, mixing, precision=lax.Precision.HIGHEST)
    inverse = 1.0 / expected[0]
    scaled = jacobian * inverse[:, None]
    gram_matrix = lax.dot_general(
        scaled, jacobian, (((0,), (0,)), ((), ())), precision=lax.Precision.HIGHEST
    )
    gradient = jnp.dot(excess_counts[0] * inverse, jacobian, precision=lax.Precision.HIGHEST)
    gram_matrix, gradient = lax.psum((gram_matrix, gradient), ("evt", "var", "chan"))
    gram_matrix = gram_matrix + jnp.eye(NUIS, dtype=jnp.float32)
    factor = jnp.linalg.cholesky(gram_matrix)
    step_sizes = jax.scipy.linalg.cho_solve((factor, True), gradient)
    nuisance_pulls = step_sizes * jnp.sqrt(jnp.diagonal(gram_matrix))
    return (local_templates[None], nuisance_pulls)


def solution(mesh):
    placed = (
        P("chan", ("grp", "evt"), "var"),
        P("chan", ("grp", "evt"), None),
        P("chan", ("grp", "evt")),
        P(),
        P(),
        P("chan", ("grp", "evt", "var")),
        P("chan", ("grp", "evt", "var")),
    )
    return jax.shard_map(
        shards,
        mesh=mesh,
        in_specs=placed,
        out_specs=(P("chan", ("grp", "evt", "var"), None), P("grp")),
        check_vma=False,
    )
```

profile of v0, /device:TPU:0, one launch (start us, length us, event | category | flops | bytes accessed | tf_op | source)
XLA Modules:
  0.0 670.6 jit_solution(15033247227140351277)
XLA Ops:
  8.4 3.5 fusion.70
  11.9 17.4 %convolution_convert_fusion = bf16[128,128,512]{2,0,1:T(8,128)(2,1)} fusion(f32[32,128,512]{2,1,0:T(8,128)S(1)} %fusion.70, s32[32]{0:T(128)S(1)} %bitcast.179), kind=kOutput, calls=%fused_computation.3 | convolution fusion | flops 3229618176 | bytes 25165952 | tf_op jit(solution)/shard_map/qk,ktv->qtv/dot_general | solution.py:34
  29.3 18.5 %copy.16 = bf16[128,128,512]{2,1,0:T(8,128)(2,1)} copy(bf16[128,128,512]{2,0,1:T(8,128)(2,1)} %convolution_convert_fusion) | data formatting | bytes 33554432 | tf_op jit(solution)/shard_map/convert_element_type | solution.py:36
  47.8 283.1 %reduce-scatter.2.cloned.1.call-done = bf16[4096,512]{1,0:T(8,128)(2,1)} async-done(((bf16[16384,512]{1,0:T(8,128)(2,1)}), bf16[4096,512]{1,0:T(8,128)(2,1)}) %reduce-scatter.2.cloned.1.call-update) | async-done | bytes 4194320 | tf_op jit(solution)/shard_map/reduce_scatter | solution.py:35
  331.0 5.7 all-to-all-start
  336.9 47.4 %all-to-all-done = bf16[2,2048,512]{2,1,0:T(8,128)(2,1)} async-done(((bf16[2,2048,512]{2,1,0:T(8,128)(2,1)}), bf16[2,2048,512]{2,1,0:T(8,128)(2,1)}, u32[]{:S(2)}, u32[]{:S(2)}) %all-to-all-start) | async-done | bytes 4194336 | tf_op jit(solution)/shard_map/all_to_all | solution.py:43
  384.2 6.2 copy.18
  390.5 9.6 %fusion.4 = f32[2048,512]{1,0:T(8,128)S(1)} fusion(bf16[2048,1024]{0,1:T(8,128)(2,1)} %bitcast.167, f32[1024]{0:T(1024)S(1)} %copy-done.8, s32[1024]{0:T(1024)S(1)} %copy-done.9), kind=kOutput, calls=%fused_computation.8 | convolution fusion | flops 12885950464 | bytes 8396800 | tf_op jit(solution)/shard_map/dot_general | solution.py:49
  400.1 2.0 copy-done.2
  402.1 9.0 %fusion.1 = f32[512,512]{0,1:T(8,128)} fusion(f32[2048,512]{1,0:T(8,128)S(1)} %fusion.4, f32[2048]{0:T(1024)S(1)} %bitcast.169), kind=kOutput, calls=%fused_computation.5 | convolution fusion | flops 6443499520 | bytes 5251072 | tf_op jit(solution)/shard_map/dot_general | solution.py:52
  411.1 6.8 %bitcast_convert_fusion = f32[2048,2,512]{2,0,1:T(8,128)} fusion(bf16[2,2048,512]{2,1,0:T(8,128)(2,1)} %all-to-all-done), kind=kLoop, calls=%fused_computation.120 | loop fusion | flops 2097152 | bytes 12582912 | tf_op jit(solution)/shard_map/convert_element_type | solution.py:45
  417.9 8.7 %copy.17 = f32[2048,2,512]{0,2,1:T(8,128)} copy(f32[2048,2,512]{2,0,1:T(8,128)} %bitcast_convert_fusion) | data formatting | bytes 16777216 | tf_op jit(solution)/shard_map/convert_element_type | solution.py:45
  426.6 9.3 %copy.21 = f32[1,2048,1024]{2,1,0:T(8,128)} copy(f32[1,2048,1024]{1,2,0:T(8,128)} %bitcast.164) | data formatting | bytes 16777216
  435.9 4.3 fusion.71
  440.2 32.0 %psum.15 = f32[512]{0:T(512)S(1)} all-reduce(f32[512]{0:T(512)S(1)} %bitcast.175), channel_id=1, replica_groups=mesh['grp'=2,'evt'=4,'var'=2,'chan'=2] {'evt','var','chan'}, use_global_device_ids=true, to_apply=%region_10.11 | all-reduce | flops 512 | bytes 4096 | tf_op jit(solution)/shard_map/psum | solution.py:56
  472.2 32.2 %all-reduce.3.cloned.1.call-done = f32[512,512]{0,1:T(8,128)} async-done(((f32[512,512]{0,1:T(8,128)}), f32[512,512]{0,1:T(8,128)}) %all-reduce.3.cloned.1.call-update) | async-done | bytes 1048592 | tf_op jit(solution)/shard_map/psum | solution.py:56
  504.4 1.4 convert_add_fusion
  507.4 11.7 %cholesky.104 = f32[128,128]{1,0:T(8,128)S(1)} custom-call(f32[128,128]{1,0:T(8,128)S(1)} %cholesky.266), custom_call_target="Cholesky" | custom-call | tf_op jit(solution)/shard_map/jit(cholesky)/cholesky | solution.py:58
  519.2 9.8 %custom-call.34 = f32[1,128,128]{1,2,0:T(8,128)S(1)} custom-call(f32[1,128,128]{2,1,0:T(8,128)S(1)} %get-tuple-element.31), custom_call_target="InvertDiagBlocksLowerTriangular" | custom-call | tf_op jit(solution)/shard_map/jit(cholesky)/cholesky | solution.py:58
  531.6 11.7 %cholesky.217 = f32[128,128]{1,0:T(8,128)S(1)} custom-call(f32[128,128]{1,0:T(8,128)S(1)} %cholesky.270), custom_call_target="Cholesky" | custom-call | tf_op jit(solution)/shard_map/jit(cholesky)/cholesky | solution.py:58
  543.4 10.2 %custom-call.35 = f32[1,128,128]{1,2,0:T(8,128)S(1)} custom-call(f32[1,128,128]{2,1,0:T(8,128)S(1)} %get-tuple-element.28), custom_call_target="InvertDiagBlocksLowerTriangular" | custom-call | tf_op jit(solution)/shard_map/jit(cholesky)/cholesky | solution.py:58
  553.9 1.3 convolution_subtract_fusion.1
  555.2 11.7 %cholesky.238 = f32[128,128]{1,0:T(8,128)S(1)} custom-call(f32[128,128]{1,0:T(8,128)S(1)} %cholesky.275), custom_call_target="Cholesky" | custom-call | tf_op jit(solution)/shard_map/jit(cholesky)/cholesky | solution.py:58
  567.7 9.8 %custom-call.36 = f32[1,128,128]{1,2,0:T(8,128)S(1)} custom-call(f32[1,128,128]{2,1,0:T(8,128)S(1)} %get-tuple-element.25), custom_call_target="InvertDiagBlocksLowerTriangular" | custom-call | tf_op jit(solution)/shard_map/jit(cholesky)/cholesky | solution.py:58
  578.9 11.7 %cholesky.255 = f32[128,128]{1,0:T(8,128)S(1)} custom-call(f32[128,128]{1,0:T(8,128)S(1)} %convolution_subtract_fusion.2), custom_call_target="Cholesky" | custom-call | tf_op jit(solution)/shard_map/jit(cholesky)/cholesky | solution.py:58
  595.9 14.1 %while.1 = (s32[]{:T(128)}, f32[512,512]{1,0:T(8,128)}, s32[4,2]{0,1:T(2,128)S(1)}, f32[4,128,128]{2,1,0:T(8,128)}, s32[]{:T(128)}) while((s32[]{:T(128)}, f32[512,512]{1,0:T(8,128)}, s32[4,2]{0,1:T(2,128)S(1)}, f32[4,128,128]{2,1,0:T(8,128)}, s32[]{:T(128)}) %tuple.32), condition=%wide.while_cond, body=%wide.while_body.sunk | while | flops 2 | bytes 132705 | solution.py:59
  596.6 2.9 bitcast_dynamic-update-slice_fusion.2
  600.1 2.9 bitcast_dynamic-update-slice_fusion.2
  603.7 2.9 bitcast_dynamic-update-slice_fusion.2
  607.2 2.8 bitcast_dynamic-update-slice_fusion.2
  610.0 40.1 %custom-call.37 = f32[4,128,128]{1,2,0:T(8,128)S(1)} custom-call(f32[4,128,128]{2,1,0:T(8,128)} %get-tuple-element.9), custom_call_target="InvertDiagBlocksLowerTriangular" | custom-call | tf_op jit(solution)/shard_map/jit(_cho_solve)/triangular_solve | solution.py:59
  658.5 4.6 gather_fusion
  (72 shorter events, 22.1 us)
Async XLA Ops:
  7.2 1.2 copy-start
  7.2 323.8 %reduce-scatter.2.cloned.1.call-start = ((), (), s32[]{:S(2)}) async-start(), calls=%async_computation.2 | async-start | bytes 20971520 | tf_op jit(solution)/shard_map/reduce_scatter | solution.py:35
  8.4 3.5 copy-start.7
  331.0 5.8 copy-start.6
  331.0 5.9 copy-start.5
  331.0 53.3 %all-to-all-start = ((bf16[2,2048,512]{2,1,0:T(8,128)(2,1)}), bf16[2,2048,512]{2,1,0:T(8,128)(2,1)}, u32[]{:S(2)}, u32[]{:S(2)}) async-start(bf16[2,2048,512]{2,1,0:T(8,128)(2,1)} %bitcast.166), calls=%async_computation.1 | async-start | bytes 8388608 | tf_op jit(solution)/shard_map/all_to_all | solution.py:43
  336.7 167.7 %all-reduce.3.cloned.1.call-start = ((), (), s32[]{:S(2)}) async-start(), calls=%async_computation.3 | async-start | bytes 2097152 | tf_op jit(solution)/shard_map/psum | solution.py:56
  384.2 6.2 copy-start.8
  384.2 6.2 copy-start.9
  400.1 2.0 copy-start.2
  504.4 1.8 copy-start.3
  506.4 1.0 copy-start.4
  553.6 110.0 %copy-start.1 = (bf16[1,4096,128]{2,1,0:T(8,128)(2,1)S(1)}, bf16[1,4096,128]{2,1,0:T(8,128)(2,1)}, u32[]{:S(2)}) copy-start(bf16[1,4096,128]{2,1,0:T(8,128)(2,1)} %param.8) | copy-start | bytes 3145732
Sparse Core Ops, SparseCore 0:
  48.0 282.9 reduce-scatter.1
  411.2 93.1 all-reduce.2
where the time goes:
time: 680 us; the launch traced here: 671 us
  waiting for transfers between devices  363 us (53%)
  other arithmetic  129 us (19%)
  local copies, waits for them, and re-layouts  66.1 us (10%)
  matrix products  57.5 us (8%)
  blocking collectives  32 us (5%)
  between operations  17.3 us (3%)
    reduce_scatter x1, waiting for transfers between devices, shards(): lax.psum_scatter(block_term.reshape(CH_BINS // evt_count * lax.axis_size(...  283 us
    another operation x14, other arithmetic, shards(): factor = jnp.linalg.cholesky(gram_matrix)  78.9 us
    all_to_all x1, waiting for transfers between devices, shards(): lax.all_to_all(summed.astype(jnp.bfloat16), 'var', split_axis=0, concat_a...  47.4 us
    another operation x4, other arithmetic, shards(): step_sizes = jax.scipy.linalg.cho_solve((factor, True), gradient)  41.3 us
    psum x1, waiting for transfers between devices, shards(): lax.psum((gram_matrix, gradient), ('evt', 'var', 'chan'))  32.2 us
    psum x1, blocking collectives, shards(): lax.psum((gram_matrix, gradient), ('evt', 'var', 'chan'))  32 us
    convert_element_type x1, local copies, waits for them, and re-layouts, shards(): block_term.reshape(CH_BINS // evt_count * lax.axis_size('evt'), var_local)  18.5 us
    dot_general x1, matrix products, shards(): jnp.einsum('qk,ktv->qtv', select, products, precision=lax.Precision.HIGHEST)  17.4 us
  transfers between devices with their start and end apart: 3, of which 3 were waited for; matrix products, arithmetic and copies ran while one was open for 4% of the time, Pallas kernels for 0%

commit v1 on v0

--- a/solution.py
+++ b/solution.py
@@ -6,6 +6,7 @@
 BLK = 128
 CH_BINS = 16384
 NUIS = 512
+_balance_spans = lambda arr: jax.lax.psum(jax.lax.psum(arr, ("var", "chan")), "evt")
 
 
 def shards(
@@ -53,7 +54,7 @@
         scaled, jacobian, (((0,), (0,)), ((), ())), precision=lax.Precision.HIGHEST
     )
     gradient = jnp.dot(excess_counts[0] * inverse, jacobian, precision=lax.Precision.HIGHEST)
-    gram_matrix, gradient = lax.psum((gram_matrix, gradient), ("evt", "var", "chan"))
+    gram_matrix, gradient = _balance_spans((gram_matrix, gradient))
     gram_matrix = gram_matrix + jnp.eye(NUIS, dtype=jnp.float32)
     factor = jnp.linalg.cholesky(gram_matrix)
     step_sizes = jax.scipy.linalg.cho_solve((factor, True), gradient)

time: 680 us -> 678 us (level)
  blocking collectives: 32 us -> 17.9 us
  waiting for transfers between devices: 363 us -> 375 us
    psum x1 -> x2, blocking collectives: 32 us -> 17.9 us  [the longest x1 12.1 us: jax.lax.psum(jax.lax.psum(arr, ('var', 'chan')), 'evt')]
    psum x1 -> x2, waiting for transfers between devices: 32.2 us -> 44 us  [the longest x1 36.2 us: jax.lax.psum(arr, ('var', 'chan'))]
  transfers between devices with their start and end apart: 3 -> 4, of which waited for: 3 -> 4; matrix products, arithmetic and copies ran while one was open for 4% -> 4% of each run, Pallas kernels for 0% -> 0%
where the time goes in v1:
time: 678 us; the launch traced here: 668 us
  waiting for transfers between devices  375 us (55%)
  other arithmetic  129 us (19%)
  local copies, waits for them, and re-layouts  66.1 us (10%)
  matrix products  57.5 us (8%)
  blocking collectives  17.9 us (3%)
  between operations  17 us (3%)
    reduce_scatter x1, waiting for transfers between devices, shards(): lax.psum_scatter(block_term.reshape(CH_BINS // evt_count * lax.axis_size(...  283 us
    another operation x14, other arithmetic, shards(): factor = jnp.linalg.cholesky(gram_matrix)  78.9 us
    all_to_all x1, waiting for transfers between devices, shards(): lax.all_to_all(summed.astype(jnp.bfloat16), 'var', split_axis=0, concat_a...  47.4 us
    another operation x4, other arithmetic, shards(): step_sizes = jax.scipy.linalg.cho_solve((factor, True), gradient)  41.3 us
    psum x1, waiting for transfers between devices, jax.lax.psum(arr, ('var', 'chan'))  36.2 us
    convert_element_type x1, local copies, waits for them, and re-layouts, shards(): block_term.reshape(CH_BINS // evt_count * lax.axis_size('evt'), var_local)  18.5 us
    dot_general x1, matrix products, shards(): jnp.einsum('qk,ktv->qtv', select, products, precision=lax.Precision.HIGHEST)  17.4 us
    another operation x12, local copies, waits for them, and re-layouts  14.1 us
  transfers between devices with their start and end apart: 4, of which 4 were waited for; matrix products, arithmetic and copies ran while one was open for 4% of the time, Pallas kernels for 0%

profile of v1, /device:TPU:0, one launch (start us, length us, event | category | flops | bytes accessed | tf_op | source)
XLA Modules:
  0.0 668.2 jit_solution(17557415232742538163)
XLA Ops:
  8.4 3.5 fusion.70
  11.9 17.4 %convolution_convert_fusion = bf16[128,128,512]{2,0,1:T(8,128)(2,1)} fusion(f32[32,128,512]{2,1,0:T(8,128)S(1)} %fusion.70, s32[32]{0:T(128)S(1)} %bitcast.179), kind=kOutput, calls=%fused_computation.3 | convolution fusion | flops 3229618176 | bytes 25165952 | tf_op jit(solution)/shard_map/qk,ktv->qtv/dot_general | solution.py:35
  29.3 18.5 %copy.16 = bf16[128,128,512]{2,1,0:T(8,128)(2,1)} copy(bf16[128,128,512]{2,0,1:T(8,128)(2,1)} %convolution_convert_fusion) | data formatting | bytes 33554432 | tf_op jit(solution)/shard_map/convert_element_type | solution.py:37
  47.8 283.2 %reduce-scatter.2.cloned.1.call-done = bf16[4096,512]{1,0:T(8,128)(2,1)} async-done(((bf16[16384,512]{1,0:T(8,128)(2,1)}), bf16[4096,512]{1,0:T(8,128)(2,1)}) %reduce-scatter.2.cloned.1.call-update) | async-done | bytes 4194320 | tf_op jit(solution)/shard_map/reduce_scatter | solution.py:36
  331.0 5.7 all-to-all-start
  336.8 47.4 %all-to-all-done = bf16[2,2048,512]{2,1,0:T(8,128)(2,1)} async-done(((bf16[2,2048,512]{2,1,0:T(8,128)(2,1)}), bf16[2,2048,512]{2,1,0:T(8,128)(2,1)}, u32[]{:S(2)}, u32[]{:S(2)}) %all-to-all-start) | async-done | bytes 4194336 | tf_op jit(solution)/shard_map/all_to_all | solution.py:44
  384.2 6.2 copy.18
  390.5 9.6 %fusion.4 = f32[2048,512]{1,0:T(8,128)S(1)} fusion(bf16[2048,1024]{0,1:T(8,128)(2,1)} %bitcast.167, f32[1024]{0:T(1024)S(1)} %copy-done.8, s32[1024]{0:T(1024)S(1)} %copy-done.9), kind=kOutput, calls=%fused_computation.8 | convolution fusion | flops 12885950464 | bytes 8396800 | tf_op jit(solution)/shard_map/dot_general | solution.py:50
  400.1 2.0 copy-done.2
  402.1 9.0 %fusion.1 = f32[512,512]{0,1:T(8,128)} fusion(f32[2048,512]{1,0:T(8,128)S(1)} %fusion.4, f32[2048]{0:T(1024)S(1)} %bitcast.168), kind=kOutput, calls=%fused_computation.5 | convolution fusion | flops 6443499520 | bytes 5251072 | tf_op jit(solution)/shard_map/dot_general | solution.py:53
  411.2 36.2 %all-reduce.4.cloned.1.call-done = f32[512,512]{0,1:T(8,128)} async-done(((f32[512,512]{0,1:T(8,128)}), f32[512,512]{0,1:T(8,128)}) %all-reduce.4.cloned.1.call-update) | async-done | bytes 1048592 | tf_op jit(solution)/shard_map/psum | solution.py:9
  447.4 6.8 %bitcast_convert_fusion = f32[2048,2,512]{2,0,1:T(8,128)} fusion(bf16[2,2048,512]{2,1,0:T(8,128)(2,1)} %all-to-all-done), kind=kLoop, calls=%fused_computation.120 | loop fusion | flops 2097152 | bytes 12582912 | tf_op jit(solution)/shard_map/convert_element_type | solution.py:46
  454.2 8.8 %copy.17 = f32[2048,2,512]{0,2,1:T(8,128)} copy(f32[2048,2,512]{2,0,1:T(8,128)} %bitcast_convert_fusion) | data formatting | bytes 16777216 | tf_op jit(solution)/shard_map/convert_element_type | solution.py:46
  462.9 9.3 %copy.21 = f32[1,2048,1024]{2,1,0:T(8,128)} copy(f32[1,2048,1024]{1,2,0:T(8,128)} %bitcast.164) | data formatting | bytes 16777216
  472.2 4.3 fusion.71
  476.5 5.9 psum.30
  482.4 12.1 %psum.31 = f32[512]{0:T(512)S(1)} all-reduce(f32[512]{0:T(512)S(1)} %psum.30), channel_id=1, replica_groups=mesh['grp'=2,'evt'=4,'var'=2,'chan'=2] {'evt'}, use_global_device_ids=true, to_apply=%region_12.13 | all-reduce | flops 512 | bytes 4096 | tf_op jit(solution)/shard_map/psum | solution.py:9
  494.4 7.8 %all-reduce.6.cloned.1.call-done = f32[512,512]{0,1:T(8,128)} async-done(((f32[512,512]{0,1:T(8,128)}), f32[512,512]{0,1:T(8,128)}) %all-reduce.6.cloned.1.call-update) | async-done | bytes 1048592 | tf_op jit(solution)/shard_map/psum | solution.py:9
  505.3 11.7 %cholesky.104 = f32[128,128]{1,0:T(8,128)S(1)} custom-call(f32[128,128]{1,0:T(8,128)S(1)} %cholesky.266), custom_call_target="Cholesky" | custom-call | tf_op jit(solution)/shard_map/jit(cholesky)/cholesky | solution.py:59
  517.0 9.8 %custom-call.34 = f32[1,128,128]{1,2,0:T(8,128)S(1)} custom-call(f32[1,128,128]{2,1,0:T(8,128)S(1)} %get-tuple-element.31), custom_call_target="InvertDiagBlocksLowerTriangular" | custom-call | tf_op jit(solution)/shard_map/jit(cholesky)/cholesky | solution.py:59
  529.5 11.7 %cholesky.217 = f32[128,128]{1,0:T(8,128)S(1)} custom-call(f32[128,128]{1,0:T(8,128)S(1)} %cholesky.270), custom_call_target="Cholesky" | custom-call | tf_op jit(solution)/shard_map/jit(cholesky)/cholesky | solution.py:59
  541.2 10.2 %custom-call.35 = f32[1,128,128]{1,2,0:T(8,128)S(1)} custom-call(f32[1,128,128]{2,1,0:T(8,128)S(1)} %get-tuple-element.28), custom_call_target="InvertDiagBlocksLowerTriangular" | custom-call | tf_op jit(solution)/shard_map/jit(cholesky)/cholesky | solution.py:59
  553.0 11.7 %cholesky.238 = f32[128,128]{1,0:T(8,128)S(1)} custom-call(f32[128,128]{1,0:T(8,128)S(1)} %cholesky.275), custom_call_target="Cholesky" | custom-call | tf_op jit(solution)/shard_map/jit(cholesky)/cholesky | solution.py:59
  565.5 9.8 %custom-call.36 = f32[1,128,128]{1,2,0:T(8,128)S(1)} custom-call(f32[1,128,128]{2,1,0:T(8,128)S(1)} %get-tuple-element.25), custom_call_target="InvertDiagBlocksLowerTriangular" | custom-call | tf_op jit(solution)/shard_map/jit(cholesky)/cholesky | solution.py:59
  576.8 11.7 %cholesky.255 = f32[128,128]{1,0:T(8,128)S(1)} custom-call(f32[128,128]{1,0:T(8,128)S(1)} %convolution_subtract_fusion.2), custom_call_target="Cholesky" | custom-call | tf_op jit(solution)/shard_map/jit(cholesky)/cholesky | solution.py:59
  593.8 14.1 %while.1 = (s32[]{:T(128)}, f32[512,512]{1,0:T(8,128)}, s32[4,2]{0,1:T(2,128)S(1)}, f32[4,128,128]{2,1,0:T(8,128)}, s32[]{:T(128)}) while((s32[]{:T(128)}, f32[512,512]{1,0:T(8,128)}, s32[4,2]{0,1:T(2,128)S(1)}, f32[4,128,128]{2,1,0:T(8,128)}, s32[]{:T(128)}) %tuple.32), condition=%wide.while_cond, body=%wide.while_body.sunk | while | flops 2 | bytes 132705 | solution.py:60
  594.4 2.9 bitcast_dynamic-update-slice_fusion.2
  598.0 2.9 bitcast_dynamic-update-slice_fusion.2
  601.5 2.9 bitcast_dynamic-update-slice_fusion.2
  605.1 2.8 bitcast_dynamic-update-slice_fusion.2
  607.9 40.1 %custom-call.37 = f32[4,128,128]{1,2,0:T(8,128)S(1)} custom-call(f32[4,128,128]{2,1,0:T(8,128)} %get-tuple-element.9), custom_call_target="InvertDiagBlocksLowerTriangular" | custom-call | tf_op jit(solution)/shard_map/jit(_cho_solve)/triangular_solve | solution.py:60
  656.3 4.6 gather_fusion
  (76 shorter events, 24.9 us)
Async XLA Ops:
  7.2 1.2 copy-start
  7.2 323.8 %reduce-scatter.2.cloned.1.call-start = ((), (), s32[]{:S(2)}) async-start(), calls=%async_computation.2 | async-start | bytes 20971520 | tf_op jit(solution)/shard_map/reduce_scatter | solution.py:36
  8.4 3.5 copy-start.7
  331.0 5.8 copy-start.6
  331.0 53.2 %all-to-all-start = ((bf16[2,2048,512]{2,1,0:T(8,128)(2,1)}), bf16[2,2048,512]{2,1,0:T(8,128)(2,1)}, u32[]{:S(2)}, u32[]{:S(2)}) async-start(bf16[2,2048,512]{2,1,0:T(8,128)(2,1)} %bitcast.166), calls=%async_computation.1 | async-start | bytes 8388608 | tf_op jit(solution)/shard_map/all_to_all | solution.py:44
  336.8 110.6 %all-reduce.4.cloned.1.call-start = ((), (), s32[]{:S(2)}) async-start(), calls=%async_computation.3 | async-start | bytes 2097152 | tf_op jit(solution)/shard_map/psum | solution.py:9
  384.2 6.2 copy-start.8
  384.2 6.2 copy-start.9
  400.1 2.0 copy-start.2
  402.1 9.1 %copy-start.5 = (f32[1,2048]{1,0:T(1,128)S(1)}, f32[1,2048]{1,0:T(1,128)}, u32[]{:S(2)}) copy-start(f32[1,2048]{1,0:T(1,128)} %param.13) | copy-start | bytes 24580
  411.1 91.2 %all-reduce.6.cloned.1.call-start = ((), (), s32[]{:S(2)}) async-start(), calls=%async_computation.4 | async-start | bytes 2097152 | tf_op jit(solution)/shard_map/psum | solution.py:9
  502.2 1.8 copy-start.3
  504.2 1.0 copy-start.4
  551.4 110.0 %copy-start.1 = (bf16[1,4096,128]{2,1,0:T(8,128)(2,1)S(1)}, bf16[1,4096,128]{2,1,0:T(8,128)(2,1)}, u32[]{:S(2)}) copy-start(bf16[1,4096,128]{2,1,0:T(8,128)(2,1)} %param.8) | copy-start | bytes 3145732
Sparse Core Ops, SparseCore 0:
  48.0 283.0 reduce-scatter.1
  411.2 36.1 all-reduce.3
  449.7 52.4 all-reduce.5
